TPU v7x, 256 devices: a whole 4x4x8 slice. The times are simulated.
256 devices in a mesh: sector: 8 (over y, core), inner: 32 (over x, z).
Axes of the slice: x: 4, y: 4, z: 8, core: 2. Of those that a mesh axis runs over, the one named last changes fastest.
Arguments:
- density: float32 [128, 64, 16384], P('inner', None, 'sector'), may hold values from -6 to 6
- source_sector: int32 [32, 8, 16], P('inner'), may hold values from 0 to 7, as said below
- source_tile: int32 [32, 8, 16], P('inner'), may hold values from 0 to 15
- matrix_id: int32 [32, 8, 16], P('inner'), may hold values from 0 to 31
- cubic_weights: float32 [32, 128, 128], replicated, may hold values from -0.6 to 1.5, as said below
- bin_cells: int32 [8, 32], P('sector'), may hold values from 1 to 128, 2048 in all within a row
- wave_level: float32 [8, 32], P('sector'), may hold values from 0.15 to 1
- energy_rate: float32 [128, 64], replicated, may hold values from 0.01 to 0.12
- pitch_rate: float32 [128, 64], replicated, may hold values from 0.01 to 0.12
Outputs:
- advanced: float32 [128, 64, 16384], P('inner', None, 'sector')
Inputs may be any that keep to these rules, and one draw needn't show every extreme that they name: `source_sector`: for every energy block and destination sector, at most 3 of its 16 tiles depart from any one sector, exactly 3 depart from one sector, and that sector lies one to three sectors below the destination, cyclically. `cubic_weights`: every row of every matrix sums to one.
All inputs are finite; a program needn't handle non-finite values.
Results may differ from a plain program's by a relative error of at most 0.000096.
Values sent between devices are 32-bit elements; how exact they have to be, the bound alone decides.
A program may use at most 128 MiB of HBM per device.

v0:
```python
import jax
import jax.numpy as jnp
from jax import lax
from jax.sharding import PartitionSpec as P

PASSES = 12


def order_within(sources):
    tile_count = sources.shape[1]
    same = sources[:, :, None] == sources[:, None, :]
    earlier = jnp.arange(tile_count)[None, :] < jnp.arange(tile_count)[:, None]
    return jnp.sum((same & earlier[None]).astype(jnp.int32), axis=2)


def drift_step(density, source_sector, source_tile, matrix_id, cubic_weights):
    sectors = lax.axis_size("sector")
    sector_here = lax.axis_index("sector")
    energies, pitches, cell_count = density.shape
    tile_len = cubic_weights.shape[1]
    tile_count = cell_count // tile_len
    slot_count = max(2, (3 * tile_count + 2 * sectors - 1) // (2 * sectors))
    sources = source_sector[0]
    picked_tiles = source_tile[0]
    matrix_ids = matrix_id[0]
    tile_ranks = order_within(sources)
    slot_rank = jnp.arange(slot_count, dtype=jnp.int32)
    matched = (sources[:, None, :] == sector_here) & (
        tile_ranks[:, None, :] == slot_rank[None, :, None]
    )
    chosen = jnp.sum(jnp.where(matched, picked_tiles[:, None, :], 0), axis=2).reshape(-1)
    filled = jnp.any(matched, axis=2).reshape(-1).astype(jnp.float32)
    blocks = density.reshape(energies, pitches, tile_count, tile_len)
    outgoing = jnp.take(blocks, chosen, axis=2) * filled[None, None, :, None]
    incoming = lax.all_to_all(outgoing, "sector", split_axis=2, concat_axis=2, tiled=True)
    own_sources = sources[sector_here]
    own_ranks = tile_ranks[sector_here]
    own_ids = matrix_ids[sector_here]
    where_from = own_sources * slot_count + own_ranks
    departing = jnp.take(incoming, where_from, axis=2)
    matrices = jnp.take(cubic_weights, own_ids, axis=0)
    drifted = jnp.einsum("eptj,tij->epti", departing, matrices, precision=lax.Precision.HIGHEST)
    return drifted.reshape(energies, pitches, cell_count)


def one_pass(field, rate_cell, energy_rate, pitch_rate):
    flux_e = energy_rate[:-1, :, None] * (field[1:] - field[:-1])
    flux_p = pitch_rate[:, :-1, None] * (field[:, 1:] - field[:, :-1])
    change_e = jnp.pad(flux_e, ((0, 1), (0, 0), (0, 0))) - jnp.pad(flux_e, ((1, 0), (0, 0), (0, 0)))
    change_p = jnp.pad(flux_p, ((0, 0), (0, 1), (0, 0))) - jnp.pad(flux_p, ((0, 0), (1, 0), (0, 0)))
    return field + rate_cell[None, None, :] * (change_e + change_p)


def shards(
    density,
    source_sector,
    source_tile,
    matrix_id,
    cubic_weights,
    bin_cells,
    wave_level,
    energy_rate,
    pitch_rate,
):
    first = drift_step(density, source_sector, source_tile, matrix_id, cubic_weights)
    inner_count = lax.axis_size("inner")
    inner_here = lax.axis_index("inner")
    cell_count = first.shape[2]
    lengths = bin_cells[0]
    per_device = cell_count // inner_count
    owner_cells = jnp.full((inner_count,), per_device, jnp.int32)
    owner_ends = jnp.cumsum(owner_cells)
    owner_starts = owner_ends - owner_cells
    offsets = jnp.arange(per_device, dtype=jnp.int32)
    cell_index = owner_starts[:, None] + offsets[None, :]
    valid = (offsets[None, :] < owner_cells[:, None]).reshape(-1).astype(jnp.float32)
    clipped = jnp.minimum(cell_index, cell_count - 1).reshape(-1)
    packed = jnp.take(first, clipped, axis=2) * valid[None, None, :]
    cellwise = lax.all_to_all(packed, "inner", split_axis=2, concat_axis=0, tiled=True)
    bin_ends = jnp.cumsum(lengths)
    global_cells = owner_starts[inner_here] + offsets
    is_live = (offsets < owner_cells[inner_here]).astype(jnp.float32)
    bin_of = jnp.sum((bin_ends[None, :] <= global_cells[:, None]).astype(jnp.int32), axis=1)
    onehot = bin_of[:, None] == jnp.arange(inner_count, dtype=jnp.int32)[None, :]
    cell_level = jnp.sum(jnp.where(onehot, wave_level[0][None, :], 0.0), axis=1) * is_live

    def loop_body(step, current):
        return one_pass(current, cell_level, energy_rate, pitch_rate)

    diffused = lax.fori_loop(0, PASSES, loop_body, cellwise)
    returned = lax.all_to_all(diffused, "inner", split_axis=0, concat_axis=2, tiled=True)
    every_cell = jnp.arange(cell_count, dtype=jnp.int32)
    owner_index = jnp.sum((owner_ends[None, :] <= every_cell[:, None]).astype(jnp.int32), axis=1)
    offset = every_cell - owner_starts[owner_index]
    position = owner_index * per_device + offset
    restored = jnp.take(returned, position, axis=2)
    return drift_step(restored, source_sector, source_tile, matrix_id, cubic_weights)


def solution(mesh):
    return jax.shard_map(
        shards,
        mesh=mesh,
        in_specs=(
            P("inner", None, "sector"),
            P("inner", None, None),
            P("inner", None, None),
            P("inner", None, None),
            P(),
            P("sector", None),
            P("sector", None),
            P(),
            P(),
        ),
        out_specs=P("inner", None, "sector"),
        check_vma=False,
    )
```

profile of v0, /device:TPU:1, one launch (start us, length us, event | category | flops | bytes accessed | tf_op | source)
XLA Modules:
  0.0 494.0 jit_solution(5908928833812959469)
XLA Ops:
  13.2 7.6 %all-to-all-start = ((f32[4,64,24,128]{3,1,0,2:T(8,128)}), f32[4,64,24,128]{3,1,0,2:T(8,128)}, u32[]{:S(2)}, u32[]{:S(2)}) async-start(f32[4,64,24,128]{3,1,0,2:T(8,128)} %bitcast_multiply_fusion.2), calls=%async_computation | async-start | bytes 6291456 | tf_op jit(solution)/shard_map/all_to_all | solution.py:35
  23.2 35.2 %all-to-all-done = f32[4,64,24,128]{3,1,0,2:T(8,128)} async-done(((f32[4,64,24,128]{3,1,0,2:T(8,128)}), f32[4,64,24,128]{3,1,0,2:T(8,128)}, u32[]{:S(2)}, u32[]{:S(2)}) %all-to-all-start) | async-done | bytes 3145760 | tf_op jit(solution)/shard_map/all_to_all | solution.py:35
  70.5 17.5 %gather_fusion.3 = f32[2048,4,64]{2,1,0:T(4,128)} fusion(f32[4,64,2048]{1,0,2:T(4,128)} %bitcast.121, s32[2048]{0:T(1024)S(1)} %fusion.11), kind=kCustom, calls=%fused_computation.3.clone | custom fusion | bytes 4202496 | tf_op jit(solution)/shard_map/jit(_take)/gather | solution.py:78
  88.0 11.7 %fusion.21 = f32[2048,4,64]{2,1,0:T(4,128)} fusion(f32[2048]{0:T(1024)S(1)} %convert_element_type.47, f32[2048,4,64]{2,1,0:T(4,128)} %gather_fusion.3, pred[2048]{0:T(1024)(128)(4,1)S(1)} %compare_and_fusion.1), kind=kLoop, calls=%fused_computation.105 | loop fusion | flops 1048576 | bytes 4204544
  99.7 6.3 %reshape.380 = f32[32,1,16384]{2,1,0:T(1,128)} reshape(f32[2048,4,64]{2,1,0:T(4,128)} %fusion.21) | data formatting | bytes 4194304
  106.0 9.8 %all-to-all-start.1 = ((f32[32,1,16384]{2,1,0:T(1,128)}), f32[32,1,16384]{2,1,0:T(1,128)S(1)}, u32[]{:S(2)}, u32[]{:S(2)}) async-start(f32[32,1,16384]{2,1,0:T(1,128)} %reshape.380), calls=%async_computation.1 | async-start | bytes 4194304 | tf_op jit(solution)/shard_map/all_to_all | solution.py:79
  117.9 46.4 %all-to-all-done.1 = f32[32,1,16384]{2,1,0:T(1,128)S(1)} async-done(((f32[32,1,16384]{2,1,0:T(1,128)}), f32[32,1,16384]{2,1,0:T(1,128)S(1)}, u32[]{:S(2)}, u32[]{:S(2)}) %all-to-all-start.1) | async-done | bytes 2097184 | tf_op jit(solution)/shard_map/all_to_all | solution.py:79
  166.1 7.3 %reduce.51 = f32[32,16384]{1,0:T(8,128)S(1)} reduce(f32[32,1,16384]{2,1,0:T(1,128)} %copy-done.4, f32[]{:T(128)} %broadcast.519), dimensions={1}, to_apply=%all_to_all.33.reduce_sub_computation | reduce | bytes 4194308 | tf_op jit(solution)/shard_map/all_to_all | solution.py:79
  177.7 5.2 %copy.57 = f32[4,64,32,64]{3,1,0,2:T(8,128)} copy(f32[4,64,32,64]{1,0,3,2:T(4,128)} %bitcast.119) | data formatting | bytes 4194304 | tf_op jit(solution)/shard_map/all_to_all | solution.py:79
  182.9 146.8 %while.12 = (s32[]{:T(128)}, f32[128,64,64]{2,1,0:T(8,128)}, f32[64]{0:T(128)S(1)}, f32[128,64]{1,0:T(8,128)S(1)}, f32[128,64]{1,0:T(8,128)S(1)}, /*index=5*/s32[]{:T(128)}) while((s32[]{:T(128)}, f32[128,64,64]{2,1,0:T(8,128)}, f32[64]{0:T(128)S(1)}, f32[128,64]{1,0:T(8,128)S(1)}, f32[128,64]{1,0:T(8,128)S(1)}, /*index=5*/s32[]{:T(128)}) %tuple.96), condition=%wide.region_7.12_spmd, body=%wide.region_6.11_spmd.sunk | while | flops 4694018 | bytes 37617276 | solution.py:90
  182.9 5.5 %subtract_multiply_fusion.4 = f32[128,63,64]{2,1,0:T(8,128)S(1)} fusion(f32[128,64,64]{2,1,0:T(8,128)} %get-tuple-element.209, f32[128,63]{1,0:T(8,128)S(1)} %bitcast.128), kind=kLoop, calls=%fused_computation.8.clone.1 | loop fusion | flops 1032192 | bytes 6225408 | tf_op jit(solution)/shard_map/while/body/eval_jaxpr/mul | solution.py:48
  195.1 5.5 %subtract_multiply_fusion.4 = f32[128,63,64]{2,1,0:T(8,128)S(1)} fusion(f32[128,64,64]{2,1,0:T(8,128)} %get-tuple-element.209, f32[128,63]{1,0:T(8,128)S(1)} %bitcast.128), kind=kLoop, calls=%fused_computation.8.clone.1 | loop fusion | flops 1032192 | bytes 6225408 | tf_op jit(solution)/shard_map/while/body/eval_jaxpr/mul | solution.py:48
  207.4 5.5 %subtract_multiply_fusion.4 = f32[128,63,64]{2,1,0:T(8,128)S(1)} fusion(f32[128,64,64]{2,1,0:T(8,128)} %get-tuple-element.209, f32[128,63]{1,0:T(8,128)S(1)} %bitcast.128), kind=kLoop, calls=%fused_computation.8.clone.1 | loop fusion | flops 1032192 | bytes 6225408 | tf_op jit(solution)/shard_map/while/body/eval_jaxpr/mul | solution.py:48
  219.6 5.5 %subtract_multiply_fusion.4 = f32[128,63,64]{2,1,0:T(8,128)S(1)} fusion(f32[128,64,64]{2,1,0:T(8,128)} %get-tuple-element.209, f32[128,63]{1,0:T(8,128)S(1)} %bitcast.128), kind=kLoop, calls=%fused_computation.8.clone.1 | loop fusion | flops 1032192 | bytes 6225408 | tf_op jit(solution)/shard_map/while/body/eval_jaxpr/mul | solution.py:48
  231.8 5.5 %subtract_multiply_fusion.4 = f32[128,63,64]{2,1,0:T(8,128)S(1)} fusion(f32[128,64,64]{2,1,0:T(8,128)} %get-tuple-element.209, f32[128,63]{1,0:T(8,128)S(1)} %bitcast.128), kind=kLoop, calls=%fused_computation.8.clone.1 | loop fusion | flops 1032192 | bytes 6225408 | tf_op jit(solution)/shard_map/while/body/eval_jaxpr/mul | solution.py:48
  244.1 5.5 %subtract_multiply_fusion.4 = f32[128,63,64]{2,1,0:T(8,128)S(1)} fusion(f32[128,64,64]{2,1,0:T(8,128)} %get-tuple-element.209, f32[128,63]{1,0:T(8,128)S(1)} %bitcast.128), kind=kLoop, calls=%fused_computation.8.clone.1 | loop fusion | flops 1032192 | bytes 6225408 | tf_op jit(solution)/shard_map/while/body/eval_jaxpr/mul | solution.py:48
  256.3 5.5 %subtract_multiply_fusion.4 = f32[128,63,64]{2,1,0:T(8,128)S(1)} fusion(f32[128,64,64]{2,1,0:T(8,128)} %get-tuple-element.209, f32[128,63]{1,0:T(8,128)S(1)} %bitcast.128), kind=kLoop, calls=%fused_computation.8.clone.1 | loop fusion | flops 1032192 | bytes 6225408 | tf_op jit(solution)/shard_map/while/body/eval_jaxpr/mul | solution.py:48
  268.5 5.5 %subtract_multiply_fusion.4 = f32[128,63,64]{2,1,0:T(8,128)S(1)} fusion(f32[128,64,64]{2,1,0:T(8,128)} %get-tuple-element.209, f32[128,63]{1,0:T(8,128)S(1)} %bitcast.128), kind=kLoop, calls=%fused_computation.8.clone.1 | loop fusion | flops 1032192 | bytes 6225408 | tf_op jit(solution)/shard_map/while/body/eval_jaxpr/mul | solution.py:48
  280.8 5.5 %subtract_multiply_fusion.4 = f32[128,63,64]{2,1,0:T(8,128)S(1)} fusion(f32[128,64,64]{2,1,0:T(8,128)} %get-tuple-element.209, f32[128,63]{1,0:T(8,128)S(1)} %bitcast.128), kind=kLoop, calls=%fused_computation.8.clone.1 | loop fusion | flops 1032192 | bytes 6225408 | tf_op jit(solution)/shard_map/while/body/eval_jaxpr/mul | solution.py:48
  293.0 5.5 %subtract_multiply_fusion.4 = f32[128,63,64]{2,1,0:T(8,128)S(1)} fusion(f32[128,64,64]{2,1,0:T(8,128)} %get-tuple-element.209, f32[128,63]{1,0:T(8,128)S(1)} %bitcast.128), kind=kLoop, calls=%fused_computation.8.clone.1 | loop fusion | flops 1032192 | bytes 6225408 | tf_op jit(solution)/shard_map/while/body/eval_jaxpr/mul | solution.py:48
  305.3 5.5 %subtract_multiply_fusion.4 = f32[128,63,64]{2,1,0:T(8,128)S(1)} fusion(f32[128,64,64]{2,1,0:T(8,128)} %get-tuple-element.209, f32[128,63]{1,0:T(8,128)S(1)} %bitcast.128), kind=kLoop, calls=%fused_computation.8.clone.1 | loop fusion | flops 1032192 | bytes 6225408 | tf_op jit(solution)/shard_map/while/body/eval_jaxpr/mul | solution.py:48
  317.5 5.5 %subtract_multiply_fusion.4 = f32[128,63,64]{2,1,0:T(8,128)S(1)} fusion(f32[128,64,64]{2,1,0:T(8,128)} %get-tuple-element.209, f32[128,63]{1,0:T(8,128)S(1)} %bitcast.128), kind=kLoop, calls=%fused_computation.8.clone.1 | loop fusion | flops 1032192 | bytes 6225408 | tf_op jit(solution)/shard_map/while/body/eval_jaxpr/mul | solution.py:48
  329.7 5.5 %reshape.382 = f32[32,1,16384]{2,1,0:T(1,128)} reshape(f32[128,64,64]{2,1,0:T(8,128)} %get-tuple-element.74) | data formatting | bytes 4194304
  335.2 7.5 %all-to-all-start.2 = ((f32[32,1,16384]{2,1,0:T(1,128)}), f32[32,1,16384]{2,1,0:T(1,128)}, u32[]{:S(2)}, u32[]{:S(2)}) async-start(f32[32,1,16384]{2,1,0:T(1,128)} %reshape.382), calls=%async_computation.2 | async-start | bytes 4194304 | tf_op jit(solution)/shard_map/all_to_all | solution.py:91
  343.5 4.5 compare_select_fusion.1
  348.6 15.5 %compare_and_fusion = (pred[2048]{0:T(1024)(128)(4,1)S(1)}, s32[2048]{0:T(1024)S(1)}) fusion(pred[2048]{0:T(1024)(128)(4,1)S(1)} %get-tuple-element.119, pred[2048]{0:T(1024)(128)(4,1)S(1)} %get-tuple-element.118, pred[2048]{0:T(1024)(128)(4,1)S(1)} %get-tuple-element.117, pred[2048]{0:T(1024)(128)(4,1)S(1)} %get-tuple-element.116, ...), kind=kLoop, calls=%fused_computation.74 | loop fusion | flops 69632 | bytes 77924 | tf_op jit(solution)/shard_map/jit(_take)/and | solution.py:96
  364.1 27.0 %all-to-all-done.2 = f32[32,1,16384]{2,1,0:T(1,128)} async-done(((f32[32,1,16384]{2,1,0:T(1,128)}), f32[32,1,16384]{2,1,0:T(1,128)}, u32[]{:S(2)}, u32[]{:S(2)}) %all-to-all-start.2) | async-done | bytes 2097184 | tf_op jit(solution)/shard_map/all_to_all | solution.py:91
  391.1 7.3 %reduce.52 = f32[32,16384]{1,0:T(8,128)S(1)} reduce(f32[32,1,16384]{2,1,0:T(1,128)} %all-to-all-done.2, f32[]{:T(128)} %broadcast.519), dimensions={1}, to_apply=%all_to_all.37.reduce_sub_computation | reduce | bytes 4194308 | tf_op jit(solution)/shard_map/all_to_all | solution.py:91
  401.5 5.2 %copy.58 = f32[4,64,32,64]{1,0,3,2:T(4,128)} copy(f32[4,64,32,64]{3,1,0,2:T(8,128)} %bitcast.120) | data formatting | bytes 4194304 | tf_op jit(solution)/shard_map/all_to_all | solution.py:91
  406.7 17.5 %gather_fusion.4 = f32[2048,4,64]{2,1,0:T(4,128)} fusion(f32[4,64,2048]{1,0,2:T(4,128)} %bitcast.122, s32[2048]{0:T(1024)S(1)} %broadcast_clamp_fusion), kind=kCustom, calls=%fused_computation.6.clone | custom fusion | bytes 4202496 | tf_op jit(solution)/shard_map/jit(_take)/gather | solution.py:96
  424.2 10.9 %broadcast_select_fusion = f32[2048,4,64]{2,1,0:T(4,128)} fusion(f32[2048,4,64]{2,1,0:T(4,128)} %gather_fusion.4, pred[2048]{0:T(1024)(128)(4,1)S(1)} %get-tuple-element.130), kind=kLoop, calls=%fused_computation.15 | loop fusion | flops 524288 | bytes 4196352 | tf_op jit(solution)/shard_map/jit(_take)/select_n | solution.py:96
  443.4 42.2 %all_to_all.46 = f32[4,64,24,128]{3,1,0,2:T(8,128)S(1)} all-to-all(f32[4,64,24,128]{3,1,0,2:T(8,128)S(1)} %bitcast_multiply_fusion.1), channel_id=1, replica_groups=mesh['sector'=8,'inner'=32] {'sector'}, dimensions={2} | all-to-all | bytes 6291456 | tf_op jit(solution)/shard_map/all_to_all | solution.py:35
  (148 shorter events, 137.2 us)
Async XLA Ops:
  0.0 3.1 copy-start
  13.2 8.6 %copy-start.5 = (f32[32,128,128]{2,1,0:T(8,128)S(1)}, f32[32,128,128]{2,1,0:T(8,128)}, u32[]{:S(2)}) copy-start(f32[32,128,128]{2,1,0:T(8,128)} %param.23) | copy-start | bytes 6291460
  13.2 45.2 %all-to-all-start = ((f32[4,64,24,128]{3,1,0,2:T(8,128)}), f32[4,64,24,128]{3,1,0,2:T(8,128)}, u32[]{:S(2)}, u32[]{:S(2)}) async-start(f32[4,64,24,128]{3,1,0,2:T(8,128)} %bitcast_multiply_fusion.2), calls=%async_computation | async-start | bytes 6291456 | tf_op jit(solution)/shard_map/all_to_all | solution.py:35
  106.0 9.8 %copy-start.8 = (s32[1,32]{1,0:T(1,128)S(1)}, s32[1,32]{1,0:T(1,128)}, u32[]{:S(2)}) copy-start(s32[1,32]{1,0:T(1,128)} %param.24) | copy-start | bytes 388
  106.0 10.1 %copy-start.6 = (f32[128,64]{0,1:T(8,128)S(1)}, f32[128,64]{0,1:T(8,128)}, u32[]{:S(2)}) copy-start(f32[128,64]{0,1:T(8,128)} %param.26) | copy-start | bytes 98308
  106.0 10.2 %copy-start.7 = (f32[128,64]{0,1:T(8,128)S(1)}, f32[128,64]{0,1:T(8,128)}, u32[]{:S(2)}) copy-start(f32[128,64]{0,1:T(8,128)} %param.27) | copy-start | bytes 98308
  106.0 11.8 %copy-start.9 = (f32[1,32]{1,0:T(1,128)S(1)}, f32[1,32]{1,0:T(1,128)}, u32[]{:S(2)}) copy-start(f32[1,32]{1,0:T(1,128)} %param.25) | copy-start | bytes 388
  106.0 58.3 %all-to-all-start.1 = ((f32[32,1,16384]{2,1,0:T(1,128)}), f32[32,1,16384]{2,1,0:T(1,128)S(1)}, u32[]{:S(2)}, u32[]{:S(2)}) async-start(f32[32,1,16384]{2,1,0:T(1,128)} %reshape.380), calls=%async_computation.1 | async-start | bytes 4194304 | tf_op jit(solution)/shard_map/all_to_all | solution.py:79
  182.9 5.5 %copy-start.2 = (f32[128,64,64]{2,1,0:T(8,128)S(1)}, f32[128,64,64]{2,1,0:T(8,128)}, u32[]{:S(2)}) copy-start(f32[128,64,64]{2,1,0:T(8,128)} %get-tuple-element.209) | copy-start | bytes 6291460 | tf_op jit(solution)/shard_map/while
  193.2 1.9 copy-start.3
  195.1 5.5 %copy-start.2 = (f32[128,64,64]{2,1,0:T(8,128)S(1)}, f32[128,64,64]{2,1,0:T(8,128)}, u32[]{:S(2)}) copy-start(f32[128,64,64]{2,1,0:T(8,128)} %get-tuple-element.209) | copy-start | bytes 6291460 | tf_op jit(solution)/shard_map/while
  205.4 1.9 copy-start.3
  207.4 5.5 %copy-start.2 = (f32[128,64,64]{2,1,0:T(8,128)S(1)}, f32[128,64,64]{2,1,0:T(8,128)}, u32[]{:S(2)}) copy-start(f32[128,64,64]{2,1,0:T(8,128)} %get-tuple-element.209) | copy-start | bytes 6291460 | tf_op jit(solution)/shard_map/while
  217.7 1.9 copy-start.3
  219.6 5.5 %copy-start.2 = (f32[128,64,64]{2,1,0:T(8,128)S(1)}, f32[128,64,64]{2,1,0:T(8,128)}, u32[]{:S(2)}) copy-start(f32[128,64,64]{2,1,0:T(8,128)} %get-tuple-element.209) | copy-start | bytes 6291460 | tf_op jit(solution)/shard_map/while
  229.9 1.9 copy-start.3
  231.8 5.5 %copy-start.2 = (f32[128,64,64]{2,1,0:T(8,128)S(1)}, f32[128,64,64]{2,1,0:T(8,128)}, u32[]{:S(2)}) copy-start(f32[128,64,64]{2,1,0:T(8,128)} %get-tuple-element.209) | copy-start | bytes 6291460 | tf_op jit(solution)/shard_map/while
  242.1 1.9 copy-start.3
  244.1 5.5 %copy-start.2 = (f32[128,64,64]{2,1,0:T(8,128)S(1)}, f32[128,64,64]{2,1,0:T(8,128)}, u32[]{:S(2)}) copy-start(f32[128,64,64]{2,1,0:T(8,128)} %get-tuple-element.209) | copy-start | bytes 6291460 | tf_op jit(solution)/shard_map/while
  254.4 1.9 copy-start.3
  256.3 5.5 %copy-start.2 = (f32[128,64,64]{2,1,0:T(8,128)S(1)}, f32[128,64,64]{2,1,0:T(8,128)}, u32[]{:S(2)}) copy-start(f32[128,64,64]{2,1,0:T(8,128)} %get-tuple-element.209) | copy-start | bytes 6291460 | tf_op jit(solution)/shard_map/while
  266.6 1.9 copy-start.3
  268.5 5.5 %copy-start.2 = (f32[128,64,64]{2,1,0:T(8,128)S(1)}, f32[128,64,64]{2,1,0:T(8,128)}, u32[]{:S(2)}) copy-start(f32[128,64,64]{2,1,0:T(8,128)} %get-tuple-element.209) | copy-start | bytes 6291460 | tf_op jit(solution)/shard_map/while
  278.9 1.9 copy-start.3
  280.8 5.5 %copy-start.2 = (f32[128,64,64]{2,1,0:T(8,128)S(1)}, f32[128,64,64]{2,1,0:T(8,128)}, u32[]{:S(2)}) copy-start(f32[128,64,64]{2,1,0:T(8,128)} %get-tuple-element.209) | copy-start | bytes 6291460 | tf_op jit(solution)/shard_map/while
  291.1 1.9 copy-start.3
  293.0 5.5 %copy-start.2 = (f32[128,64,64]{2,1,0:T(8,128)S(1)}, f32[128,64,64]{2,1,0:T(8,128)}, u32[]{:S(2)}) copy-start(f32[128,64,64]{2,1,0:T(8,128)} %get-tuple-element.209) | copy-start | bytes 6291460 | tf_op jit(solution)/shard_map/while
  305.3 5.5 %copy-start.2 = (f32[128,64,64]{2,1,0:T(8,128)S(1)}, f32[128,64,64]{2,1,0:T(8,128)}, u32[]{:S(2)}) copy-start(f32[128,64,64]{2,1,0:T(8,128)} %get-tuple-element.209) | copy-start | bytes 6291460 | tf_op jit(solution)/shard_map/while
  315.6 1.9 copy-start.3
  317.5 5.5 %copy-start.2 = (f32[128,64,64]{2,1,0:T(8,128)S(1)}, f32[128,64,64]{2,1,0:T(8,128)}, u32[]{:S(2)}) copy-start(f32[128,64,64]{2,1,0:T(8,128)} %get-tuple-element.209) | copy-start | bytes 6291460 | tf_op jit(solution)/shard_map/while
  335.2 55.9 %all-to-all-start.2 = ((f32[32,1,16384]{2,1,0:T(1,128)}), f32[32,1,16384]{2,1,0:T(1,128)}, u32[]{:S(2)}, u32[]{:S(2)}) async-start(f32[32,1,16384]{2,1,0:T(1,128)} %reshape.382), calls=%async_computation.2 | async-start | bytes 4194304 | tf_op jit(solution)/shard_map/all_to_all | solution.py:91
  490.3 3.7 copy-start.1
  (3 other events, 5.2 us)
where the time goes:
time: 496 us; the launch traced here: 494 us
  other arithmetic  194 us (39%)
  local copies, waits for them, and re-layouts  120 us (24%)
  waiting for transfers between devices  109 us (22%)
  blocking collectives  42.2 us (9%)
  starting transfers between devices  24.9 us (5%)
    mul x12, other arithmetic, one_pass(): flux_p = pitch_rate[:, :-1, None] * (field[:, 1:] - field[:, :-1])  65.8 us
    all_to_all x1, waiting for transfers between devices, shards(): lax.all_to_all(packed, 'inner', split_axis=2, concat_axis=0, tiled=True)  46.4 us
    all_to_all x1, blocking collectives, drift_step(): lax.all_to_all(outgoing, 'sector', split_axis=2, concat_axis=2, tiled=True)  42.2 us
    add x12, other arithmetic, one_pass(): return field + rate_cell[None, None, :] * (change_e + change_p)  35.7 us
    all_to_all x1, waiting for transfers between devices, drift_step(): lax.all_to_all(outgoing, 'sector', split_axis=2, concat_axis=2, tiled=True)  35.2 us
    all_to_all x1, waiting for transfers between devices, shards(): lax.all_to_all(diffused, 'inner', split_axis=0, concat_axis=2, tiled=True)  27 us
    while x48, local copies, waits for them, and re-layouts  23.1 us
    mul x12, other arithmetic, one_pass(): flux_e = energy_rate[:-1, :, None] * (field[1:] - field[:-1])  21.8 us
  transfers between devices with their start and end apart: 3, of which 3 were waited for; matrix products, arithmetic and copies ran while one was open for 5% of the time, Pallas kernels for 0%

commit v1 on v0

--- a/solution.py
+++ b/solution.py
@@ -4,6 +4,13 @@
 from jax.sharding import PartitionSpec as P
 
 PASSES = 12
+
+
+def trade_parts(x, axis, split, join):
+    n_dev = lax.axis_size(axis)
+    blocks = jnp.stack(jnp.split(x, n_dev, axis=split), axis=0)
+    blocks = lax.all_to_all(blocks, axis, split_axis=0, concat_axis=0)
+    return jnp.concatenate(blocks, axis=join)
 
 
 def order_within(sources):
@@ -76,7 +83,7 @@
     valid = (offsets[None, :] < owner_cells[:, None]).reshape(-1).astype(jnp.float32)
     clipped = jnp.minimum(cell_index, cell_count - 1).reshape(-1)
     packed = jnp.take(first, clipped, axis=2) * valid[None, None, :]
-    cellwise = lax.all_to_all(packed, "inner", split_axis=2, concat_axis=0, tiled=True)
+    cellwise = trade_parts(packed, "inner", 2, 0)
     bin_ends = jnp.cumsum(lengths)
     global_cells = owner_starts[inner_here] + offsets
     is_live = (offsets < owner_cells[inner_here]).astype(jnp.float32)

time: 496 us -> 494 us (level)
  blocking collectives: 42.2 us -> 99.1 us
  waiting for transfers between devices: 109 us -> 59.3 us
  starting transfers between devices: 24.9 us -> 17.1 us
  other arithmetic: 194 us -> 188 us
    all_to_all x0 -> x1, blocking collectives: none -> 54.6 us  [shards(): lax.all_to_all(diffused, 'inner', split_axis=0, concat_axis=2, tiled=True)]
    mul x12, other arithmetic: 65.8 us -> 17 us  [one_pass(): flux_p = pitch_rate[:, :-1, None] * (field[:, 1:] - field[:, :-1])]
    mul x12, other arithmetic: 21.8 us -> 65.6 us  [one_pass(): flux_e = energy_rate[:-1, :, None] * (field[1:] - field[:-1])]
    all_to_all x2 -> x1, waiting for transfers between devices: 73.4 us -> 47.2 us  [trade_parts(): blocks = lax.all_to_all(blocks, axis, split_axis=0, concat_axis=0)]
    all_to_all x1, waiting for transfers between devices: 35.2 us -> 12.1 us  [drift_step(): lax.all_to_all(outgoing, 'sector', split_axis=2, concat_axis=2, tiled=True)]
    unnamed x1 -> x0, other arithmetic: 11.7 us -> none
    mul x0 -> x1, other arithmetic: none -> 10.9 us  [shards(): packed = jnp.take(first, clipped, axis=2) * valid[None, None, :]]
    all_to_all x2 -> x1, starting transfers between devices: 17.2 us -> 9.63 us  [trade_parts(): blocks = lax.all_to_all(blocks, axis, split_axis=0, concat_axis=0)]
  transfers between devices with their start and end apart: 3 -> 2, of which waited for: 3 -> 2; matrix products, arithmetic and copies ran while one was open for 5% -> 5% of each run, Pallas kernels for 0% -> 0%
where the time goes in v1:
time: 494 us; the launch traced here: 492 us
  other arithmetic  188 us (38%)
  local copies, waits for them, and re-layouts  123 us (25%)
  blocking collectives  99.1 us (20%)
  waiting for transfers between devices  59.3 us (12%)
  starting transfers between devices  17.1 us (3%)
    mul x12, other arithmetic, one_pass(): flux_e = energy_rate[:-1, :, None] * (field[1:] - field[:-1])  65.6 us
    all_to_all x1, blocking collectives, shards(): lax.all_to_all(diffused, 'inner', split_axis=0, concat_axis=2, tiled=True)  54.6 us
    all_to_all x1, waiting for transfers between devices, trade_parts(): blocks = lax.all_to_all(blocks, axis, split_axis=0, concat_axis=0)  47.2 us
    all_to_all x1, blocking collectives, drift_step(): lax.all_to_all(outgoing, 'sector', split_axis=2, concat_axis=2, tiled=True)  44.5 us
    add x12, other arithmetic, one_pass(): return field + rate_cell[None, None, :] * (change_e + change_p)  35.7 us
    while x48, local copies, waits for them, and re-layouts  23.1 us
    unnamed x51, local copies, waits for them, and re-layouts  22 us
    gather x1, local copies, waits for them, and re-layouts, shards(): packed = jnp.take(first, clipped, axis=2) * valid[None, None, :]  17.5 us
  transfers between devices with their start and end apart: 2, of which 2 were waited for; matrix products, arithmetic and copies ran while one was open for 5% of the time, Pallas kernels for 0%

profile of v1, /device:TPU:1, one launch (start us, length us, event | category | flops | bytes accessed | tf_op | source)
XLA Modules:
  0.0 491.8 jit_solution(6471826953418503344)
XLA Ops:
  9.6 4.3 bitcast_multiply_fusion.2
  13.9 7.5 %all-to-all-start = ((f32[4,64,24,128]{3,1,0,2:T(8,128)}), f32[4,64,24,128]{3,1,0,2:T(8,128)}, u32[]{:S(2)}, u32[]{:S(2)}) async-start(f32[4,64,24,128]{3,1,0,2:T(8,128)} %bitcast_multiply_fusion.2), calls=%async_computation | async-start | bytes 6291456 | tf_op jit(solution)/shard_map/all_to_all | solution.py:42
  26.2 4.4 compare_select_fusion.1
  31.2 15.7 %compare_and_fusion = (pred[2048]{0:T(1024)(128)(4,1)S(1)}, s32[2048]{0:T(1024)S(1)}) fusion(pred[2048]{0:T(1024)(128)(4,1)S(1)} %get-tuple-element.119, pred[2048]{0:T(1024)(128)(4,1)S(1)} %get-tuple-element.118, pred[2048]{0:T(1024)(128)(4,1)S(1)} %get-tuple-element.117, pred[2048]{0:T(1024)(128)(4,1)S(1)} %get-tuple-element.116, ...), kind=kLoop, calls=%fused_computation.138 | loop fusion | flops 69632 | bytes 77924 | tf_op jit(solution)/shard_map/jit(_take)/and | solution.py:103
  46.9 12.1 %all-to-all-done = f32[4,64,24,128]{3,1,0,2:T(8,128)} async-done(((f32[4,64,24,128]{3,1,0,2:T(8,128)}), f32[4,64,24,128]{3,1,0,2:T(8,128)}, u32[]{:S(2)}, u32[]{:S(2)}) %all-to-all-start) | async-done | bytes 3145760 | tf_op jit(solution)/shard_map/all_to_all | solution.py:42
  71.1 17.5 %gather_fusion.3 = f32[2048,4,64]{2,1,0:T(4,128)} fusion(f32[4,64,2048]{1,0,2:T(4,128)} %bitcast.242, s32[2048]{0:T(1024)S(1)} %get-tuple-element.171), kind=kCustom, calls=%fused_computation.3.clone | custom fusion | bytes 4202496 | tf_op jit(solution)/shard_map/jit(_take)/gather | solution.py:85
  88.6 10.9 %bitcast_multiply_fusion = f32[4,64,2048]{1,0,2:T(4,128)S(1)} fusion(f32[2048,4,64]{2,1,0:T(4,128)} %gather_fusion.3, f32[2048]{0:T(1024)S(1)} %convert_element_type.47, pred[2048]{0:T(1024)(128)(4,1)S(1)} %compare_and_fusion.1), kind=kLoop, calls=%fused_computation.10 | loop fusion | flops 1048576 | bytes 4204544 | tf_op jit(solution)/shard_map/mul | solution.py:85
  102.3 6.3 %reshape.384 = f32[32,1,16384]{2,1,0:T(1,128)} reshape(f32[32,64,4,64]{3,2,1,0:T(4,128)} %bitcast.248) | data formatting | bytes 4194304
  108.6 9.6 %all-to-all-start.1 = ((f32[32,1,16384]{2,1,0:T(1,128)}), f32[32,1,16384]{2,1,0:T(1,128)S(1)}, u32[]{:S(2)}, u32[]{:S(2)}) async-start(f32[32,1,16384]{2,1,0:T(1,128)} %reshape.384), calls=%async_computation.1 | async-start | bytes 4194304 | tf_op jit(solution)/shard_map/all_to_all | solution.py:12
  119.6 47.2 %all-to-all-done.1 = f32[32,1,16384]{2,1,0:T(1,128)S(1)} async-done(((f32[32,1,16384]{2,1,0:T(1,128)}), f32[32,1,16384]{2,1,0:T(1,128)S(1)}, u32[]{:S(2)}, u32[]{:S(2)}) %all-to-all-start.1) | async-done | bytes 2097184 | tf_op jit(solution)/shard_map/all_to_all | solution.py:12
  168.6 7.4 %reduce.51 = f32[32,16384]{1,0:T(8,128)S(1)} reduce(f32[32,1,16384]{2,1,0:T(1,128)} %copy-done.4, f32[]{:T(128)} %broadcast.515), dimensions={1}, to_apply=%all_to_all.23.reduce_sub_computation | reduce | bytes 4194308 | tf_op jit(solution)/shard_map/all_to_all | solution.py:12
  180.2 5.2 %copy.43 = f32[32,4,64,64]{3,2,1,0:T(8,128)} copy(f32[32,4,64,64]{2,1,3,0:T(4,128)} %bitcast.240) | data formatting | bytes 4194304 | tf_op jit(solution)/shard_map/all_to_all | solution.py:12
  185.5 142.0 %while.12 = (s32[]{:T(128)}, f32[128,64,64]{2,1,0:T(8,128)}, f32[64]{0:T(128)S(1)}, f32[128,64]{1,0:T(8,128)S(1)}, f32[128,64]{1,0:T(8,128)S(1)}, /*index=5*/s32[]{:T(128)}) while((s32[]{:T(128)}, f32[128,64,64]{2,1,0:T(8,128)}, f32[64]{0:T(128)S(1)}, f32[128,64]{1,0:T(8,128)S(1)}, f32[128,64]{1,0:T(8,128)S(1)}, /*index=5*/s32[]{:T(128)}) %tuple.98), condition=%wide.region_7.12_spmd, body=%wide.region_6.11_spmd.sunk | while | flops 4694018 | bytes 37617276 | solution.py:97
  185.5 5.5 %subtract_multiply_fusion.5 = f32[127,64,64]{2,1,0:T(8,128)S(1)} fusion(f32[128,64,64]{2,1,0:T(8,128)} %get-tuple-element.213, f32[127,64]{1,0:T(8,128)S(1)} %bitcast.249), kind=kLoop, calls=%fused_computation.9.clone.1 | loop fusion | flops 1040384 | bytes 6274816 | tf_op jit(solution)/shard_map/while/body/eval_jaxpr/mul | solution.py:54
  197.3 5.5 %subtract_multiply_fusion.5 = f32[127,64,64]{2,1,0:T(8,128)S(1)} fusion(f32[128,64,64]{2,1,0:T(8,128)} %get-tuple-element.213, f32[127,64]{1,0:T(8,128)S(1)} %bitcast.249), kind=kLoop, calls=%fused_computation.9.clone.1 | loop fusion | flops 1040384 | bytes 6274816 | tf_op jit(solution)/shard_map/while/body/eval_jaxpr/mul | solution.py:54
  209.1 5.5 %subtract_multiply_fusion.5 = f32[127,64,64]{2,1,0:T(8,128)S(1)} fusion(f32[128,64,64]{2,1,0:T(8,128)} %get-tuple-element.213, f32[127,64]{1,0:T(8,128)S(1)} %bitcast.249), kind=kLoop, calls=%fused_computation.9.clone.1 | loop fusion | flops 1040384 | bytes 6274816 | tf_op jit(solution)/shard_map/while/body/eval_jaxpr/mul | solution.py:54
  221.0 5.5 %subtract_multiply_fusion.5 = f32[127,64,64]{2,1,0:T(8,128)S(1)} fusion(f32[128,64,64]{2,1,0:T(8,128)} %get-tuple-element.213, f32[127,64]{1,0:T(8,128)S(1)} %bitcast.249), kind=kLoop, calls=%fused_computation.9.clone.1 | loop fusion | flops 1040384 | bytes 6274816 | tf_op jit(solution)/shard_map/while/body/eval_jaxpr/mul | solution.py:54
  232.8 5.5 %subtract_multiply_fusion.5 = f32[127,64,64]{2,1,0:T(8,128)S(1)} fusion(f32[128,64,64]{2,1,0:T(8,128)} %get-tuple-element.213, f32[127,64]{1,0:T(8,128)S(1)} %bitcast.249), kind=kLoop, calls=%fused_computation.9.clone.1 | loop fusion | flops 1040384 | bytes 6274816 | tf_op jit(solution)/shard_map/while/body/eval_jaxpr/mul | solution.py:54
  244.6 5.5 %subtract_multiply_fusion.5 = f32[127,64,64]{2,1,0:T(8,128)S(1)} fusion(f32[128,64,64]{2,1,0:T(8,128)} %get-tuple-element.213, f32[127,64]{1,0:T(8,128)S(1)} %bitcast.249), kind=kLoop, calls=%fused_computation.9.clone.1 | loop fusion | flops 1040384 | bytes 6274816 | tf_op jit(solution)/shard_map/while/body/eval_jaxpr/mul | solution.py:54
  256.4 5.5 %subtract_multiply_fusion.5 = f32[127,64,64]{2,1,0:T(8,128)S(1)} fusion(f32[128,64,64]{2,1,0:T(8,128)} %get-tuple-element.213, f32[127,64]{1,0:T(8,128)S(1)} %bitcast.249), kind=kLoop, calls=%fused_computation.9.clone.1 | loop fusion | flops 1040384 | bytes 6274816 | tf_op jit(solution)/shard_map/while/body/eval_jaxpr/mul | solution.py:54
  268.3 5.5 %subtract_multiply_fusion.5 = f32[127,64,64]{2,1,0:T(8,128)S(1)} fusion(f32[128,64,64]{2,1,0:T(8,128)} %get-tuple-element.213, f32[127,64]{1,0:T(8,128)S(1)} %bitcast.249), kind=kLoop, calls=%fused_computation.9.clone.1 | loop fusion | flops 1040384 | bytes 6274816 | tf_op jit(solution)/shard_map/while/body/eval_jaxpr/mul | solution.py:54
  280.1 5.5 %subtract_multiply_fusion.5 = f32[127,64,64]{2,1,0:T(8,128)S(1)} fusion(f32[128,64,64]{2,1,0:T(8,128)} %get-tuple-element.213, f32[127,64]{1,0:T(8,128)S(1)} %bitcast.249), kind=kLoop, calls=%fused_computation.9.clone.1 | loop fusion | flops 1040384 | bytes 6274816 | tf_op jit(solution)/shard_map/while/body/eval_jaxpr/mul | solution.py:54
  291.9 5.5 %subtract_multiply_fusion.5 = f32[127,64,64]{2,1,0:T(8,128)S(1)} fusion(f32[128,64,64]{2,1,0:T(8,128)} %get-tuple-element.213, f32[127,64]{1,0:T(8,128)S(1)} %bitcast.249), kind=kLoop, calls=%fused_computation.9.clone.1 | loop fusion | flops 1040384 | bytes 6274816 | tf_op jit(solution)/shard_map/while/body/eval_jaxpr/mul | solution.py:54
  303.8 5.5 %subtract_multiply_fusion.5 = f32[127,64,64]{2,1,0:T(8,128)S(1)} fusion(f32[128,64,64]{2,1,0:T(8,128)} %get-tuple-element.213, f32[127,64]{1,0:T(8,128)S(1)} %bitcast.249), kind=kLoop, calls=%fused_computation.9.clone.1 | loop fusion | flops 1040384 | bytes 6274816 | tf_op jit(solution)/shard_map/while/body/eval_jaxpr/mul | solution.py:54
  315.6 5.5 %subtract_multiply_fusion.5 = f32[127,64,64]{2,1,0:T(8,128)S(1)} fusion(f32[128,64,64]{2,1,0:T(8,128)} %get-tuple-element.213, f32[127,64]{1,0:T(8,128)S(1)} %bitcast.249), kind=kLoop, calls=%fused_computation.9.clone.1 | loop fusion | flops 1040384 | bytes 6274816 | tf_op jit(solution)/shard_map/while/body/eval_jaxpr/mul | solution.py:54
  327.4 4.5 reshape.386
  331.9 54.6 %all_to_all.33 = f32[32,1,16384]{2,1,0:T(1,128)} all-to-all(f32[32,1,16384]{2,1,0:T(1,128)S(1)} %reshape.386), channel_id=1, replica_groups=mesh['sector'=8,'inner'=32] {'inner'}, dimensions={0} | all-to-all | bytes 4194304 | tf_op jit(solution)/shard_map/all_to_all | solution.py:98
  386.6 7.4 %reduce.52 = f32[32,16384]{1,0:T(8,128)S(1)} reduce(f32[32,1,16384]{2,1,0:T(1,128)} %all_to_all.33, f32[]{:T(128)} %broadcast.515), dimensions={1}, to_apply=%all_to_all.24.reduce_sub_computation | reduce | bytes 4194308 | tf_op jit(solution)/shard_map/all_to_all | solution.py:98
  397.0 5.2 %copy.53 = f32[4,64,32,64]{1,0,3,2:T(4,128)} copy(f32[4,64,32,64]{3,1,0,2:T(8,128)} %bitcast.241) | data formatting | bytes 4194304 | tf_op jit(solution)/shard_map/all_to_all | solution.py:98
  402.3 17.5 %gather_fusion.4 = f32[2048,4,64]{2,1,0:T(4,128)} fusion(f32[4,64,2048]{1,0,2:T(4,128)} %bitcast.243, s32[2048]{0:T(1024)S(1)} %get-tuple-element.172), kind=kCustom, calls=%fused_computation.6.clone | custom fusion | bytes 4202496 | tf_op jit(solution)/shard_map/jit(_take)/gather | solution.py:103
  419.8 10.9 %broadcast_select_fusion = f32[2048,4,64]{2,1,0:T(4,128)} fusion(f32[2048,4,64]{2,1,0:T(4,128)} %gather_fusion.4, pred[2048]{0:T(1024)(128)(4,1)S(1)} %get-tuple-element.130), kind=kLoop, calls=%fused_computation.15 | loop fusion | flops 524288 | bytes 4196352 | tf_op jit(solution)/shard_map/jit(_take)/select_n | solution.py:103
  439.0 44.5 %all_to_all.34 = f32[4,64,24,128]{3,1,0,2:T(8,128)S(1)} all-to-all(f32[4,64,24,128]{3,1,0,2:T(8,128)S(1)} %bitcast_multiply_fusion.1), channel_id=1, replica_groups=mesh['sector'=8,'inner'=32] {'sector'}, dimensions={2} | all-to-all | bytes 6291456 | tf_op jit(solution)/shard_map/all_to_all | solution.py:42
  (177 shorter events, 132.3 us)
Async XLA Ops:
  0.0 3.3 copy-start
  13.9 45.1 %all-to-all-start = ((f32[4,64,24,128]{3,1,0,2:T(8,128)}), f32[4,64,24,128]{3,1,0,2:T(8,128)}, u32[]{:S(2)}, u32[]{:S(2)}) async-start(f32[4,64,24,128]{3,1,0,2:T(8,128)} %bitcast_multiply_fusion.2), calls=%async_computation | async-start | bytes 6291456 | tf_op jit(solution)/shard_map/all_to_all | solution.py:42
  100.4 1.9 copy-start.5
  102.3 16.0 %copy-start.8 = (s32[1,32]{1,0:T(1,128)S(1)}, s32[1,32]{1,0:T(1,128)}, u32[]{:S(2)}) copy-start(s32[1,32]{1,0:T(1,128)} %param.24) | copy-start | bytes 388
  102.3 16.3 %copy-start.6 = (f32[128,64]{0,1:T(8,128)S(1)}, f32[128,64]{0,1:T(8,128)}, u32[]{:S(2)}) copy-start(f32[128,64]{0,1:T(8,128)} %param.26) | copy-start | bytes 98308
  102.3 16.4 %copy-start.7 = (f32[128,64]{0,1:T(8,128)S(1)}, f32[128,64]{0,1:T(8,128)}, u32[]{:S(2)}) copy-start(f32[128,64]{0,1:T(8,128)} %param.27) | copy-start | bytes 98308
  102.3 17.2 %copy-start.9 = (f32[1,32]{1,0:T(1,128)S(1)}, f32[1,32]{1,0:T(1,128)}, u32[]{:S(2)}) copy-start(f32[1,32]{1,0:T(1,128)} %param.25) | copy-start | bytes 388
  108.6 58.1 %all-to-all-start.1 = ((f32[32,1,16384]{2,1,0:T(1,128)}), f32[32,1,16384]{2,1,0:T(1,128)S(1)}, u32[]{:S(2)}, u32[]{:S(2)}) async-start(f32[32,1,16384]{2,1,0:T(1,128)} %reshape.384), calls=%async_computation.1 | async-start | bytes 4194304 | tf_op jit(solution)/shard_map/all_to_all | solution.py:12
  185.5 5.5 %copy-start.2 = (f32[128,64,64]{2,1,0:T(8,128)S(1)}, f32[128,64,64]{2,1,0:T(8,128)}, u32[]{:S(2)}) copy-start(f32[128,64,64]{2,1,0:T(8,128)} %get-tuple-element.213) | copy-start | bytes 6291460 | tf_op jit(solution)/shard_map/while
  195.4 1.9 copy-start.3
  197.3 5.5 %copy-start.2 = (f32[128,64,64]{2,1,0:T(8,128)S(1)}, f32[128,64,64]{2,1,0:T(8,128)}, u32[]{:S(2)}) copy-start(f32[128,64,64]{2,1,0:T(8,128)} %get-tuple-element.213) | copy-start | bytes 6291460 | tf_op jit(solution)/shard_map/while
  207.2 1.9 copy-start.3
  209.1 5.5 %copy-start.2 = (f32[128,64,64]{2,1,0:T(8,128)S(1)}, f32[128,64,64]{2,1,0:T(8,128)}, u32[]{:S(2)}) copy-start(f32[128,64,64]{2,1,0:T(8,128)} %get-tuple-element.213) | copy-start | bytes 6291460 | tf_op jit(solution)/shard_map/while
  219.0 1.9 copy-start.3
  221.0 5.5 %copy-start.2 = (f32[128,64,64]{2,1,0:T(8,128)S(1)}, f32[128,64,64]{2,1,0:T(8,128)}, u32[]{:S(2)}) copy-start(f32[128,64,64]{2,1,0:T(8,128)} %get-tuple-element.213) | copy-start | bytes 6291460 | tf_op jit(solution)/shard_map/while
  230.9 1.9 copy-start.3
  232.8 5.5 %copy-start.2 = (f32[128,64,64]{2,1,0:T(8,128)S(1)}, f32[128,64,64]{2,1,0:T(8,128)}, u32[]{:S(2)}) copy-start(f32[128,64,64]{2,1,0:T(8,128)} %get-tuple-element.213) | copy-start | bytes 6291460 | tf_op jit(solution)/shard_map/while
  242.7 1.9 copy-start.3
  244.6 5.5 %copy-start.2 = (f32[128,64,64]{2,1,0:T(8,128)S(1)}, f32[128,64,64]{2,1,0:T(8,128)}, u32[]{:S(2)}) copy-start(f32[128,64,64]{2,1,0:T(8,128)} %get-tuple-element.213) | copy-start | bytes 6291460 | tf_op jit(solution)/shard_map/while
  254.5 1.9 copy-start.3
  256.4 5.5 %copy-start.2 = (f32[128,64,64]{2,1,0:T(8,128)S(1)}, f32[128,64,64]{2,1,0:T(8,128)}, u32[]{:S(2)}) copy-start(f32[128,64,64]{2,1,0:T(8,128)} %get-tuple-element.213) | copy-start | bytes 6291460 | tf_op jit(solution)/shard_map/while
  266.3 1.9 copy-start.3
  268.3 5.5 %copy-start.2 = (f32[128,64,64]{2,1,0:T(8,128)S(1)}, f32[128,64,64]{2,1,0:T(8,128)}, u32[]{:S(2)}) copy-start(f32[128,64,64]{2,1,0:T(8,128)} %get-tuple-element.213) | copy-start | bytes 6291460 | tf_op jit(solution)/shard_map/while
  278.2 1.9 copy-start.3
  280.1 5.5 %copy-start.2 = (f32[128,64,64]{2,1,0:T(8,128)S(1)}, f32[128,64,64]{2,1,0:T(8,128)}, u32[]{:S(2)}) copy-start(f32[128,64,64]{2,1,0:T(8,128)} %get-tuple-element.213) | copy-start | bytes 6291460 | tf_op jit(solution)/shard_map/while
  290.0 1.9 copy-start.3
  291.9 5.5 %copy-start.2 = (f32[128,64,64]{2,1,0:T(8,128)S(1)}, f32[128,64,64]{2,1,0:T(8,128)}, u32[]{:S(2)}) copy-start(f32[128,64,64]{2,1,0:T(8,128)} %get-tuple-element.213) | copy-start | bytes 6291460 | tf_op jit(solution)/shard_map/while
  301.8 1.9 copy-start.3
  303.8 5.5 %copy-start.2 = (f32[128,64,64]{2,1,0:T(8,128)S(1)}, f32[128,64,64]{2,1,0:T(8,128)}, u32[]{:S(2)}) copy-start(f32[128,64,64]{2,1,0:T(8,128)} %get-tuple-element.213) | copy-start | bytes 6291460 | tf_op jit(solution)/shard_map/while
  313.7 1.9 copy-start.3
  315.6 5.5 %copy-start.2 = (f32[128,64,64]{2,1,0:T(8,128)S(1)}, f32[128,64,64]{2,1,0:T(8,128)}, u32[]{:S(2)}) copy-start(f32[128,64,64]{2,1,0:T(8,128)} %get-tuple-element.213) | copy-start | bytes 6291460 | tf_op jit(solution)/shard_map/while
  488.1 3.7 copy-start.1
  (2 other events, 3.2 us)
